TPU v7x, 128 devices: a whole 4x4x4 slice. The times are simulated.
128 devices in a mesh: flow: 8 (over y, core), link: 16 (over x, z).
Axes of the slice: x: 4, y: 4, z: 4, core: 2. Of those that a mesh axis runs over, the one named last changes fastest.
Arguments:
- route_tiles: bfloat16 [1024, 2048, 128], P('flow', 'link'), may hold values from 0 to 1, as said below
- tile_count: int32 [8, 16], P('flow', 'link'), may hold values from 16 to 128, as said below
- tile_flow: int32 [8, 2048], P('flow', 'link'), may hold values from 0 to 1023
- tile_link: int32 [8, 2048], P('flow', 'link'), may hold values from 0 to 511, as said below
- flow_class: int32 [1048576], P('flow'), may hold values from 0 to 255
- class_weight: float32 [256], replicated, may hold values from 0.25 to 4
- access_price: float32 [1048576], P('flow'), may hold values from 0.5 to 4
- capacity: float32 [1048576], P('link'), may hold values from 1 to 8
- init_price: float32 [1048576], P('link'), may hold values from 0.5 to 2
Outputs:
- flow_rate: float32 [1048576], P('flow')
- link_price: float32 [1048576], P('link')
Inputs may be any that keep to these rules, and one draw needn't show every extreme that they name: `route_tiles`: entries are 0 or 1. `tile_count`: counts follow 128 divided by 1, 2, 4 or 8; some device uses all 128 slots in every draw. `tile_link`: within one device's slots no link block repeats.
All inputs are finite; a program needn't handle non-finite values.
Results may differ from a plain program's by a relative error of at most 0.0014.
Values may be sent and summed in bfloat16 or wider, within the bound.
No kernel may reach another device: no remote copies, remote signals or barrier semaphores. Data moves between devices by JAX's collectives and lax.ppermute only.
A program may use at most 64 MiB of HBM per device.

v0:
```python
import jax
import jax.numpy as jnp
from jax import lax
from jax.sharding import PartitionSpec as P

ITERS = 2
step_size = 0.5


def on_device(
    route_tiles,
    tile_count,
    tile_flow,
    tile_link,
    flow_class,
    class_weight,
    access_price,
    capacity,
    init_price,
):
    slots = route_tiles.shape[0]
    tile = route_tiles.shape[2]
    valid = (jnp.arange(slots, dtype=jnp.int32) < tile_count[0, 0]).astype(jnp.float32)
    flow_idx = tile_flow[0]
    link_idx = tile_link[0]
    flow_blocks = access_price.shape[0] // tile
    link_blocks = capacity.shape[0] // tile
    link_cap = capacity.reshape(link_blocks, tile)
    price = init_price.reshape(link_blocks, tile)
    weight = jnp.take(class_weight, flow_class).reshape(flow_blocks, tile)
    access = access_price.reshape(flow_blocks, tile)
    rate = jnp.zeros((flow_blocks, tile), jnp.float32)
    for step in range(ITERS):
        price_b = price.astype(jnp.bfloat16)
        picked = jnp.take(price_b, link_idx, axis=0)
        term = (
            jnp.einsum("sab,sa->sb", route_tiles, picked, preferred_element_type=jnp.float32)
            * valid[:, None]
        )
        route_part = jax.ops.segment_sum(term, flow_idx, num_segments=flow_blocks)
        route_sum = lax.psum(route_part, "link")
        rate = weight / (access + route_sum)
        rate_b = rate.astype(jnp.bfloat16)
        sent = jnp.take(rate_b, flow_idx, axis=0)
        term = (
            jnp.einsum("sab,sb->sa", route_tiles, sent, preferred_element_type=jnp.float32)
            * valid[:, None]
        )
        load_part = jax.ops.segment_sum(term, link_idx, num_segments=link_blocks)
        load = lax.psum(load_part, "flow")
        price = price * jnp.exp(step_size * (load / link_cap - 1.0))
    return (rate.reshape(-1), price.reshape(-1))


def solution(mesh):
    return jax.shard_map(
        on_device,
        mesh=mesh,
        in_specs=(
            P("flow", "link", None),
            P("flow", "link"),
            P("flow", "link"),
            P("flow", "link"),
            P("flow"),
            P(),
            P("flow"),
            P("link"),
            P("link"),
        ),
        out_specs=(P("flow"), P("link")),
        check_vma=False,
    )
```

profile of v0, /device:TPU:0, one launch (start us, length us, event | category | flops | bytes accessed | tf_op | source)
XLA Modules:
  0.0 1073.4 jit_solution(16845775853648401084)
XLA Ops:
  7.2 0.0 copy-start
  7.2 0.0 copy-start.1
  7.2 0.0 all-reduce.5.cloned.1.call-start
  7.2 0.7 compare_and_fusion
  8.0 0.7 compare_select_fusion.1
  9.3 0.0 copy-start.7
  9.3 1.0 bitcast_convert_fusion
  10.3 0.7 gather_fusion.1
  11.0 0.1 select_bitcast_fusion.3
  11.1 3.4 fusion.27
  14.5 2.0 scatter_custom_fusion
  16.5 0.0 all-reduce.5.cloned.1.call-update
  16.5 0.0 all-reduce.7.cloned.1.call-start
  16.5 0.0 copy-done.10
  16.5 0.0 copy-done.7
  16.6 0.1 fusion.3
  16.7 0.0 copy-start.12
  16.7 0.0 copy-start.2
  16.7 0.0 copy-start.4
  16.7 815.4 %gather_fusion = f32[131072]{0:T(1024)S(1)} fusion(f32[256]{0:T(256)S(1)} %copy-done, s32[131072]{0:T(1024)S(1)} %fusion.3), kind=kCustom, calls=%fused_computation.4 | custom fusion | bytes 1572864 | tf_op jit(solution)/shard_map/jit(_take)/gather | solution.py:30
  832.2 0.0 copy-start.8
  832.2 0.0 copy-start.3
  832.2 0.0 copy-start.5
  832.3 0.0 all-reduce.5.cloned.1.call-done
  832.3 1.3 fusion.1
  833.6 0.7 gather_fusion.2
  834.3 0.1 select_bitcast_fusion.2
  834.4 4.4 fusion.25
  838.9 1.9 scatter_custom_fusion.1
  840.8 0.0 all-reduce.7.cloned.1.call-update
  840.8 0.0 all-reduce.9.cloned.1.call-start
  840.9 63.0 %all-reduce.7.cloned.1.call-done = f32[512,128]{1,0:T(8,128)} async-done(((f32[512,128]{1,0:T(8,128)}), f32[512,128]{1,0:T(8,128)}) %all-reduce.7.cloned.1.call-update) | async-done | bytes 262160 | tf_op jit(solution)/shard_map/psum | solution.py:50
  903.8 1.0 fusion.37
  904.9 0.8 gather_fusion.3
  905.7 0.1 select_bitcast_fusion.1
  905.8 3.4 fusion.23
  909.2 1.9 scatter_custom_fusion.2
  911.0 0.0 all-reduce.9.cloned.1.call-update
  911.1 0.0 all-reduce.11.cloned.1.call-start
  911.1 84.9 %all-reduce.9.cloned.1.call-done = f32[1024,128]{1,0:T(8,128)} async-done(((f32[1024,128]{1,0:T(8,128)}), f32[1024,128]{1,0:T(8,128)}) %all-reduce.9.cloned.1.call-update) | async-done | bytes 524304 | tf_op jit(solution)/shard_map/psum | solution.py:41
  996.1 2.1 fusion.38
  998.1 0.7 gather_fusion.4
  998.8 0.1 select_bitcast_fusion
  998.9 4.4 fusion.21
  1003.4 1.9 scatter_custom_fusion.3
  1005.3 0.0 all-reduce.11.cloned.1.call-update
  1005.3 59.8 %all-reduce.11.cloned.1.call-done = f32[512,128]{1,0:T(8,128)} async-done(((f32[512,128]{1,0:T(8,128)}), f32[512,128]{1,0:T(8,128)}) %all-reduce.11.cloned.1.call-update) | async-done | bytes 262160 | tf_op jit(solution)/shard_map/psum | solution.py:50
  1065.1 1.8 fusion.12
  (20 shorter events, 0.1 us)
Async XLA Ops:
  7.2 9.5 copy-start
  7.2 9.4 copy-start.1
  7.2 825.1 %all-reduce.5.cloned.1.call-start = ((), (), s32[]{:S(2)}) async-start(), calls=%async_computation | async-start | bytes 1048576 | tf_op jit(solution)/shard_map/psum | solution.py:41
  8.0 8.6 copy-start.10
  9.3 7.3 copy-start.7
  9.3 7.3 copy-start.9
  16.5 887.3 %all-reduce.7.cloned.1.call-start = ((), (), s32[]{:S(2)}) async-start(), calls=%async_computation.1 | async-start | bytes 524288 | tf_op jit(solution)/shard_map/psum | solution.py:50
  16.7 815.5 %copy-start.12 = (s32[1,128]{1,0:T(1,128)S(1)}, s32[1,128]{1,0:T(1,128)}, u32[]{:S(2)}) copy-start(s32[1,128]{1,0:T(1,128)} %param.15) | copy-start | bytes 1540
  16.7 815.6 %copy-start.2 = (s32[131072]{0:T(1024)S(1)}, s32[131072]{0:T(1024)}, u32[]{:S(2)}) copy-start(s32[131072]{0:T(1024)} %param.17) | copy-start | bytes 1572868
  16.7 815.6 %copy-start.4 = (f32[131072]{0:T(1024)S(1)}, f32[131072]{0:T(1024)}, u32[]{:S(2)}) copy-start(f32[131072]{0:T(1024)} %param.19) | copy-start | bytes 1572868
  832.2 6.7 copy-start.8
  832.2 71.6 %copy-start.3 = (f32[65536]{0:T(1024)S(1)}, f32[65536]{0:T(1024)}, u32[]{:S(2)}) copy-start(f32[65536]{0:T(1024)} %param.21) | copy-start | bytes 786436
  832.2 71.6 %copy-start.5 = (f32[65536]{0:T(1024)S(1)}, f32[65536]{0:T(1024)}, u32[]{:S(2)}) copy-start(f32[65536]{0:T(1024)} %param.20) | copy-start | bytes 786436
  832.3 73.4 %copy-start.11 = (pred[128]{0:T(512)(128)(4,1)S(1)}, pred[128]{0:T(512)(128)(4,1)}, u32[]{:S(2)}) copy-start(pred[128]{0:T(512)(128)(4,1)} %copy-done.10) | copy-start | bytes 388
  840.8 155.3 %all-reduce.9.cloned.1.call-start = ((), (), s32[]{:S(2)}) async-start(), calls=%async_computation.2 | async-start | bytes 1048576 | tf_op jit(solution)/shard_map/psum | solution.py:41
  911.1 154.0 %copy-start.6 = (f32[512,128]{1,0:T(8,128)S(1)}, f32[512,128]{1,0:T(8,128)}, u32[]{:S(2)}) copy-start(f32[512,128]{1,0:T(8,128)} %all-reduce.7.cloned.1.call-done) | copy-start | bytes 786436
  911.1 154.0 %all-reduce.11.cloned.1.call-start = ((), (), s32[]{:S(2)}) async-start(), calls=%async_computation.3 | async-start | bytes 524288 | tf_op jit(solution)/shard_map/psum | solution.py:50
Sparse Core Ops, SparseCore 0:
  16.6 88.2 all-reduce.4
  840.9 62.8 all-reduce.6
  911.2 84.8 all-reduce.8
  1005.4 59.6 all-reduce.10
where the time goes:
time: 1070 us
  local copies, waits for them, and re-layouts  818 us (76%)
  waiting for transfers between devices  208 us (19%)
  other arithmetic  16.7 us (2%)
  matrix products  15.6 us (1%)
  between operations  14.7 us (1%)
    gather x1, local copies, waits for them, and re-layouts, on_device(): weight = jnp.take(class_weight, flow_class).reshape(flow_blocks, tile)  815 us
    psum x2, waiting for transfers between devices, on_device(): load = lax.psum(load_part, 'flow')  123 us
    psum x2, waiting for transfers between devices, on_device(): route_sum = lax.psum(route_part, 'link')  85 us
  transfers between devices with their start and end apart: 4, of which 3 were waited for; matrix products, arithmetic and copies ran while one was open for 76% of the time, Pallas kernels for 0%

commit v1 on v0

--- a/solution.py
+++ b/solution.py
@@ -47,7 +47,7 @@
             * valid[:, None]
         )
         load_part = jax.ops.segment_sum(term, link_idx, num_segments=link_blocks)
-        load = lax.psum(load_part, "flow")
+        load = jnp.sum(jax.lax.all_gather(load_part, axis_name="flow"), 0)
         price = price * jnp.exp(step_size * (load / link_cap - 1.0))
     return (rate.reshape(-1), price.reshape(-1))
 

time: 1070 us -> 1010 us (0.944)
  waiting for transfers between devices: 208 us -> 139 us
    psum x2 -> x0, waiting for transfers between devices: 123 us -> none  [on_device(): load = lax.psum(load_part, 'flow')]
    all_gather x0 -> x2, waiting for transfers between devices: none -> 52.7 us  [on_device(): load = jnp.sum(jax.lax.all_gather(load_part, axis_name='flow'), 0)]
  transfers between devices with their start and end apart: 4 -> 4, of which waited for: 3 -> 3; matrix products, arithmetic and copies ran while one was open for 76% -> 81% of each run, Pallas kernels for 0% -> 0%
where the time goes in v1:
time: 1010 us
  local copies, waits for them, and re-layouts  818 us (81%)
  waiting for transfers between devices  139 us (14%)
  other arithmetic  18.2 us (2%)
  matrix products  15.6 us (2%)
  between operations  14.7 us (1%)
    gather x1, local copies, waits for them, and re-layouts, on_device(): weight = jnp.take(class_weight, flow_class).reshape(flow_blocks, tile)  815 us
    psum x2, waiting for transfers between devices, on_device(): route_sum = lax.psum(route_part, 'link')  86.3 us
    all_gather x2, waiting for transfers between devices, on_device(): load = jnp.sum(jax.lax.all_gather(load_part, axis_name='flow'), 0)  52.7 us
  transfers between devices with their start and end apart: 4, of which 3 were waited for; matrix products, arithmetic and copies ran while one was open for 81% of the time, Pallas kernels for 0%

profile of v1, /device:TPU:0, one launch (start us, length us, event | category | flops | bytes accessed | tf_op | source)
XLA Modules:
  0.0 1006.2 jit_solution(5227960569146404172)
XLA Ops:
  7.2 0.0 copy-start
  7.2 0.0 copy-start.1
  7.2 0.0 all-reduce.3.cloned.1.call-start
  7.2 0.7 compare_and_fusion
  8.0 0.7 compare_select_fusion.1
  9.3 0.0 copy-start.6
  9.3 1.0 bitcast_convert_fusion
  10.3 0.7 gather_fusion.1
  11.0 0.1 select_bitcast_fusion.3
  11.1 3.4 fusion.31
  14.5 2.0 scatter_custom_fusion
  16.5 0.0 all-reduce.3.cloned.1.call-update
  16.5 0.0 all-gather.5.cloned.1.call-start
  16.6 0.1 fusion.3
  16.7 0.0 copy-start.11
  16.7 0.0 copy-start.2
  16.7 0.0 copy-start.4
  16.7 815.4 %gather_fusion = f32[131072]{0:T(1024)S(1)} fusion(f32[256]{0:T(256)S(1)} %copy-done, s32[131072]{0:T(1024)S(1)} %fusion.3), kind=kCustom, calls=%fused_computation.4 | custom fusion | bytes 1572864 | tf_op jit(solution)/shard_map/jit(_take)/gather | solution.py:30
  832.2 0.0 copy-start.7
  832.2 0.0 all-reduce.3.cloned.1.call-done
  832.3 1.3 fusion.1
  833.6 0.0 copy-start.3
  833.6 0.0 copy-start.5
  833.6 0.7 gather_fusion.2
  834.3 0.1 select_bitcast_fusion.2
  834.4 4.4 fusion.29
  838.8 1.9 scatter_custom_fusion.1
  840.7 0.0 all-gather.5.cloned.1.call-update
  840.8 0.0 all-reduce.5.cloned.1.call-start
  840.8 27.9 %all-gather.5.cloned.1.call-done = f32[4096,128]{1,0:T(8,128)} async-done(((f32[512,128]{1,0:T(8,128)}), f32[4096,128]{1,0:T(8,128)}) %all-gather.5.cloned.1.call-update) | async-done | bytes 2097168 | tf_op jit(solution)/shard_map/all_gather | solution.py:50
  868.7 1.7 reduce_sum.22
  870.5 0.1 fusion.20
  870.6 0.8 gather_fusion.3
  871.4 0.1 select_bitcast_fusion.1
  871.5 3.4 fusion.27
  874.9 1.9 scatter_custom_fusion.2
  876.7 0.0 all-reduce.5.cloned.1.call-update
  876.8 0.0 all-gather.7.cloned.1.call-start
  876.8 86.3 %all-reduce.5.cloned.1.call-done = f32[1024,128]{1,0:T(8,128)} async-done(((f32[1024,128]{1,0:T(8,128)}), f32[1024,128]{1,0:T(8,128)}) %all-reduce.5.cloned.1.call-update) | async-done | bytes 524304 | tf_op jit(solution)/shard_map/psum | solution.py:41
  963.1 2.1 fusion.41
  965.1 0.7 gather_fusion.4
  965.8 0.1 select_bitcast_fusion
  965.9 4.4 fusion.25
  970.4 1.9 scatter_custom_fusion.3
  972.3 0.0 all-gather.7.cloned.1.call-update
  972.3 24.8 %all-gather.7.cloned.1.call-done = f32[4096,128]{1,0:T(8,128)} async-done(((f32[512,128]{1,0:T(8,128)}), f32[4096,128]{1,0:T(8,128)}) %all-gather.7.cloned.1.call-update) | async-done | bytes 2097168 | tf_op jit(solution)/shard_map/all_gather | solution.py:50
  997.1 1.7 reduce_sum.24
  998.8 0.8 fusion.7
  (20 shorter events, 0.1 us)
Async XLA Ops:
  7.2 9.5 copy-start
  7.2 9.4 copy-start.1
  7.2 825.1 %all-reduce.3.cloned.1.call-start = ((), (), s32[]{:S(2)}) async-start(), calls=%async_computation | async-start | bytes 1048576 | tf_op jit(solution)/shard_map/psum | solution.py:41
  8.0 8.6 copy-start.9
  9.3 7.3 copy-start.6
  9.3 7.3 copy-start.8
  16.5 852.2 %all-gather.5.cloned.1.call-start = ((), (), s32[]{:S(2)}) async-start(), calls=%async_computation.2 | async-start | bytes 2359296 | tf_op jit(solution)/shard_map/all_gather | solution.py:50
  16.7 815.5 %copy-start.11 = (s32[1,128]{1,0:T(1,128)S(1)}, s32[1,128]{1,0:T(1,128)}, u32[]{:S(2)}) copy-start(s32[1,128]{1,0:T(1,128)} %param.15) | copy-start | bytes 1540
  16.7 815.5 %copy-start.2 = (s32[131072]{0:T(1024)S(1)}, s32[131072]{0:T(1024)}, u32[]{:S(2)}) copy-start(s32[131072]{0:T(1024)} %param.17) | copy-start | bytes 1572868
  16.7 815.5 %copy-start.4 = (f32[131072]{0:T(1024)S(1)}, f32[131072]{0:T(1024)}, u32[]{:S(2)}) copy-start(f32[131072]{0:T(1024)} %param.19) | copy-start | bytes 1572868
  832.2 6.6 copy-start.7
  833.6 36.9 %copy-start.3 = (f32[65536]{0:T(1024)S(1)}, f32[65536]{0:T(1024)}, u32[]{:S(2)}) copy-start(f32[65536]{0:T(1024)} %param.21) | copy-start | bytes 786436
  833.6 36.9 %copy-start.5 = (f32[65536]{0:T(1024)S(1)}, f32[65536]{0:T(1024)}, u32[]{:S(2)}) copy-start(f32[65536]{0:T(1024)} %param.20) | copy-start | bytes 786436
  834.4 37.0 %copy-start.10 = (pred[128]{0:T(512)(128)(4,1)S(1)}, pred[128]{0:T(512)(128)(4,1)}, u32[]{:S(2)}) copy-start(pred[128]{0:T(512)(128)(4,1)} %copy-done.9) | copy-start | bytes 388
  840.8 122.3 %all-reduce.5.cloned.1.call-start = ((), (), s32[]{:S(2)}) async-start(), calls=%async_computation.1 | async-start | bytes 1048576 | tf_op jit(solution)/shard_map/psum | solution.py:41
  876.8 120.4 %all-gather.7.cloned.1.call-start = ((), (), s32[]{:S(2)}) async-start(), calls=%async_computation.3 | async-start | bytes 2359296 | tf_op jit(solution)/shard_map/all_gather | solution.py:50
Sparse Core Ops, SparseCore 0:
  16.6 88.2 all-reduce.2
  840.9 27.7 all-gather.4
  876.9 86.1 all-reduce.4
  972.4 24.6 all-gather.6
